TPU v7x, 32 devices: a whole 2x2x4 slice. The times are simulated.
32 devices in a mesh: grp: 8 (over z, core), exp: 4 (over y, x).
Axes of the slice: x: 2, y: 2, z: 4, core: 2. Of those that a mesh axis runs over, the one named last changes fastest.
Arguments:
- sky: float32 [32, 6, 8, 512], P(('grp', 'exp')), may hold values from -6 to 6
- observed: bfloat16 [128, 6, 8, 512], P(('grp', 'exp')), may hold values from -6 to 6
- intersections: int32 [128, 4], P(('grp', 'exp')), may hold values from 0 to 7
- resample_index: int32 [128, 4], P(('grp', 'exp')), may hold values from 0 to 7
- psf_index: int32 [128], P(('grp', 'exp')), may hold values from 0 to 15
- resample_table: bfloat16 [8, 512, 512], replicated, may hold values from -0.25 to 0.25
- psf_weights: float32 [16, 8], replicated, may hold values from -5 to 5
- psf_basis: float32 [8, 41], replicated, may hold values from -0.3125 to 0.3125
Outputs:
- sky_out: float32 [32, 6, 8, 512], P(('grp', 'exp'))
- residual: float32 [128, 6, 8, 512], P(('grp', 'exp'))
Inputs may be any that keep to these rules, and one draw needn't show every extreme that they name: `intersections`: with G = 4: an entry v below G names tile v of the exposure's own group; an entry v of G or more names tile v - G of the next group along grp, cyclically.
All inputs are finite; a program needn't handle non-finite values.
Results may differ from a plain program's by a relative error of at most 0.019.
Values may be sent and summed in bfloat16 or wider, within the bound.
A program may use at most 128 MiB of HBM per device.

v0:
```python
import jax
import jax.numpy as jnp
from jax import lax
from jax.sharding import PartitionSpec as P

ITERS = 2
STEP = 0.05


def shifted(block, axis, distance):
    devices = range(lax.axis_size(axis))
    route = [((i - distance) % len(devices), i) for i in devices]
    return lax.ppermute(block, axis, route)


def conv_matrices(kernels, width, taps):
    half = (taps - 1) // 2
    count = kernels.shape[0]
    head = kernels[:, half::-1]
    tail = kernels[:, taps - 1 : half : -1]
    blank = jnp.zeros((count, 2 * width - 1 - taps), jnp.float32)
    pattern = jnp.concatenate([head, blank, tail], axis=1)
    tiled = jnp.broadcast_to(pattern[:, None, :], (count, width, 2 * width - 1)).reshape(
        count, width * (2 * width - 1)
    )
    tiled = tiled[:, : width * (2 * width - 2)].reshape(count, width, 2 * width - 2)[:, :, :width]
    return tiled.astype(jnp.bfloat16)


def fetch_window(sky_half):
    own_group = lax.all_gather(sky_half, "exp", axis=0, tiled=True)
    next_group = shifted(own_group, "grp", -1)
    return jnp.concatenate([own_group, next_group], axis=0)


def return_partials(grads, group_tiles):
    own_part = grads[:group_tiles]
    next_part = grads[group_tiles:]
    arrived = shifted(next_part.astype(jnp.bfloat16), "grp", 1).astype(next_part.dtype)
    return lax.psum_scatter(
        (own_part + arrived).astype(jnp.bfloat16), "exp", scatter_dimension=0, tiled=True
    ).astype(jnp.float32)


def shards(
    sky, observed, intersections, resample_index, psf_index, resample_table, psf_weights, psf_basis
):
    exposures_here, intersection_count = intersections.shape
    group_tiles = sky.shape[0] * lax.axis_size("exp")
    width = resample_table.shape[1]
    taps = psf_basis.shape[1]
    table_rows = psf_weights.shape[0]
    res_count = resample_table.shape[0]
    selector = (
        psf_index[:, None] == lax.broadcasted_iota(jnp.int32, (exposures_here, table_rows), 1)
    ).astype(jnp.float32)
    weights = jnp.sum(selector[:, :, None] * psf_weights[None, :, :], axis=1)
    kernels = jnp.sum(weights[:, :, None] * psf_basis[None, :, :], axis=1)
    conv = conv_matrices(kernels, width, taps)
    window_iota = lax.broadcasted_iota(
        jnp.int32, (exposures_here, intersection_count, 2 * group_tiles), 2
    )
    tile_onehot = intersections[:, :, None] == window_iota
    pick_tiles = tile_onehot.astype(jnp.bfloat16)
    onehots = tile_onehot.astype(jnp.float32)
    res_iota = lax.broadcasted_iota(jnp.int32, (exposures_here, intersection_count, res_count), 2)
    pick_res = (resample_index[:, :, None] == res_iota).astype(jnp.bfloat16)
    matrices = jnp.einsum(
        "ekn,nwv->ekwv", pick_res, resample_table, preferred_element_type=jnp.float32
    ).astype(jnp.bfloat16)
    sky_out = sky
    residual = jnp.zeros(observed.shape, jnp.float32)
    for step in range(ITERS):
        window = fetch_window(sky_out.astype(jnp.bfloat16))
        chosen = jnp.einsum(
            "ekt,tbrw->ekbrw", pick_tiles, window, preferred_element_type=jnp.float32
        ).astype(jnp.bfloat16)
        pre = jnp.zeros(observed.shape, jnp.float32)
        for k in range(intersection_count):
            pre = pre + jnp.einsum(
                "ebrw,ewv->ebrv", chosen[:, k], matrices[:, k], preferred_element_type=jnp.float32
            )
        model = jnp.einsum(
            "ebrw,ewv->ebrv", pre.astype(jnp.bfloat16), conv, preferred_element_type=jnp.float32
        )
        residual = observed.astype(jnp.float32) - model
        back = jnp.einsum(
            "ebrv,ewv->ebrw",
            residual.astype(jnp.bfloat16),
            conv,
            preferred_element_type=jnp.float32,
        ).astype(jnp.bfloat16)
        grads = jnp.zeros((2 * group_tiles,) + observed.shape[1:], jnp.float32)
        for k in range(intersection_count):
            part = jnp.einsum(
                "ebrv,ewv->ebrw", back, matrices[:, k], preferred_element_type=jnp.float32
            )
            grads = grads + jnp.einsum(
                "et,ebrw->tbrw", onehots[:, k], part, precision=lax.Precision.HIGHEST
            )
        sky_out = sky_out + STEP * return_partials(grads, group_tiles)
    return (sky_out, residual)


def solution(mesh):
    in_specs = (
        P(("grp", "exp"), None, None, None),
        P(("grp", "exp"), None, None, None),
        P(("grp", "exp"), None),
        P(("grp", "exp"), None),
        P(("grp", "exp")),
        P(),
        P(),
        P(),
    )
    out_specs = (P(("grp", "exp"), None, None, None), P(("grp", "exp"), None, None, None))
    return jax.shard_map(shards, mesh=mesh, in_specs=in_specs, out_specs=out_specs, check_vma=False)
```

profile of v0, /device:TPU:0, one launch (start us, length us, event | category | flops | bytes accessed | tf_op | source)
XLA Modules:
  0.0 216.9 jit_solution(15102472466168929469)
XLA Ops:
  7.2 0.9 convert_element_type.69
  8.1 10.2 %all_gather.6 = bf16[4,6,8,512]{3,2,1,0:T(8,128)(2,1)S(1)} all-gather(bf16[1,6,8,512]{3,2,1,0:T(8,128)(2,1)S(1)} %convert_element_type.69), channel_id=1, replica_groups=mesh['grp'=8,'exp'=4] {'exp'}, dimensions={0}, use_global_device_ids=true | all-gather | bytes 245760 | tf_op jit(solution)/shard_map/all_gather | solution.py:31
  18.4 1.1 collective-permute-start
  20.3 10.1 %convolution_convert_fusion = bf16[4,4,512,512]{3,1,2,0:T(4,128)(2,1)} fusion(bf16[8,512,512]{2,1,0:T(8,128)(2,1)} %param.13, s32[4,4]{1,0:T(4,128)} %param.11), kind=kOutput, calls=%fused_computation | convolution fusion | flops 71303296 | bytes 12582976 | tf_op jit(solution)/shard_map/ekn,nwv->ekwv/dot_general | solution.py:68
  30.4 24.7 %fusion.107 = (bf16[4,1,512,512]{3,1,2,0:T(2,128)(2,1)S(1)}, bf16[4,1,512,512]{3,1,2,0:T(2,128)(2,1)S(1)}, bf16[4,1,512,512]{3,1,2,0:T(2,128)(2,1)S(1)}, bf16[4,1,512,512]{3,1,2,0:T(2,128)(2,1)S(1)}) fusion(bf16[4,4,512,512]{3,1,2,0:T(4,128)(2,1)} %convolution_convert_fusion), kind=kLoop, calls=%fused_computation.118 | loop fusion | bytes 16777216 | tf_op jit(solution)/shard_map/slice | solution.py:81
  55.7 1.9 copy.80
  57.6 1.9 copy.84
  59.5 2.0 copy.86
  62.2 2.6 %broadcast_in_dim.5 = bf16[4,512,1023]{2,1,0:T(8,128)(2,1)} broadcast(bf16[4,1023]{1,0:T(4,128)(2,1)S(1)} %maximum_convert_fusion), dimensions={0,2} | broadcast | bytes 4198392 | tf_op jit(solution)/shard_map/broadcast_in_dim | solution.py:23
  64.8 8.5 %reshape.61 = bf16[2095104]{0:T(1024)(128)(2,1)} reshape(bf16[4,512,1023]{2,1,0:T(8,128)(2,1)} %broadcast_in_dim.5) | data formatting | bytes 8380416
  73.3 5.8 %reshape.38 = bf16[4,523776]{1,0:T(4,128)(2,1)} reshape(bf16[2095104]{0:T(1024)(128)(2,1)} %reshape.61) | data formatting | bytes 8380416 | tf_op jit(solution)/shard_map/reshape | solution.py:23
  79.1 5.3 %slice.125 = bf16[4,523264]{1,0:T(4,128)(2,1)} slice(bf16[4,523776]{1,0:T(4,128)(2,1)} %reshape.38), slice={[0:4], [0:523264]} | slice | bytes 8372224 | tf_op jit(solution)/shard_map/slice | solution.py:26
  84.4 5.8 %reshape.63 = bf16[2093056]{0:T(1024)(128)(2,1)} reshape(bf16[4,523264]{1,0:T(4,128)(2,1)} %slice.125) | data formatting | bytes 8372224
  90.3 9.4 %reshape.39 = bf16[4,512,1022]{2,1,0:T(8,128)(2,1)} reshape(bf16[2093056]{0:T(1024)(128)(2,1)} %reshape.63) | data formatting | bytes 8372224 | tf_op jit(solution)/shard_map/reshape | solution.py:26
  100.2 1.7 fusion.109
  102.4 1.1 copy-done
  104.7 0.9 copy-done.7
  106.1 3.3 %convolution_convert_fusion.4 = bf16[4,6,8,512]{3,2,1,0:T(8,128)(2,1)S(1)} fusion(bf16[4,6,8,512]{3,2,1,0:T(8,128)(2,1)S(1)} %fusion.56, bf16[4,512,1022]{2,1,0:T(8,128)(2,1)} %reshape.39, bf16[4,6,8,512]{3,2,1,0:T(8,128)(2,1)S(1)} %copy-done.12), kind=kOutput, calls=%fused_computation.56 | convolution fusion | flops 201719808 | bytes 4775936 | tf_op jit(solution)/shard_map/ebrv,ewv->ebrw/dot_general | solution.py:87
  109.4 2.5 %fusion.30 = f32[4,6,8,512]{3,2,1,0:T(8,128)S(1)} fusion(bf16[4,6,8,512]{3,2,1,0:T(8,128)(2,1)S(1)} %convolution_convert_fusion.4, bf16[4,1,512,512]{3,2,1,0:T(8,128)(2,1)} %copy.80), kind=kOutput, calls=%fused_computation.32 | convolution fusion | flops 100663296 | bytes 2686976 | tf_op jit(solution)/shard_map/ebrv,ewv->ebrw/dot_general | solution.py:95
  117.5 6.9 %collective-permute-done.1 = bf16[4,6,8,512]{3,0,2,1:T(4,128)(2,1)S(1)} collective-permute-done((bf16[4,6,8,512]{3,0,2,1:T(4,128)(2,1)S(1)}, bf16[4,6,8,512]{3,0,2,1:T(4,128)(2,1)S(1)}, u32[]{:S(2)}, u32[]{:S(2)}) %collective-permute-start.1) | collective-permute-done | bytes 196640 | tf_op jit(solution)/shard_map/ppermute | solution.py:13
  125.2 21.6 %reduce-scatter.7.cloned.1.call-done = bf16[1,6,8,512]{3,2,1,0:T(8,128)(2,1)} async-done(((bf16[4,6,8,512]{3,2,1,0:T(8,128)(2,1)}), bf16[1,6,8,512]{3,2,1,0:T(8,128)(2,1)}) %reduce-scatter.7.cloned.1.call-update) | async-done | bytes 49168
  147.7 8.9 %all_gather.7 = bf16[4,6,8,512]{3,2,1,0:T(8,128)(2,1)S(1)} all-gather(bf16[1,6,8,512]{3,2,1,0:T(8,128)(2,1)S(1)} %fusion.97), channel_id=1, replica_groups=mesh['grp'=8,'exp'=4] {'exp'}, dimensions={0}, use_global_device_ids=true | all-gather | bytes 245760 | tf_op jit(solution)/shard_map/all_gather | solution.py:31
  157.2 3.2 %collective-permute-done.2 = bf16[4,6,8,512]{3,0,2,1:T(4,128)(2,1)S(1)} collective-permute-done((bf16[4,6,8,512]{3,0,2,1:T(4,128)(2,1)S(1)}, bf16[4,6,8,512]{3,0,2,1:T(4,128)(2,1)S(1)}, u32[]{:S(2)}, u32[]{:S(2)}) %collective-permute-start.2) | collective-permute-done | bytes 196640 | tf_op jit(solution)/shard_map/ppermute | solution.py:13
  160.8 1.4 fusion.108
  162.6 1.1 copy-done.1
  165.0 3.0 %convolution_subtract_fusion = f32[4,6,8,512]{3,2,1,0:T(8,128)S(1)} fusion(f32[4,6,8,512]{3,2,1,0:T(8,128)S(1)} %fusion.43, bf16[4,1,512,512]{3,2,1,0:T(8,128)(2,1)} %copy.86, bf16[4,512,1022]{2,1,0:T(8,128)(2,1)} %reshape.39, bf16[4,6,8,512]{3,2,1,0:T(8,128)(2,1)} %param.9, bf16[4,1,6,8,512]{4,1,3,2,0:T(2,128)(2,1)S(1)} %get-tuple-element.10), kind=kOutput, calls=%fused_computation.50 | convolution fusion | flops 201719808 | bytes 5373952 | tf_op jit(solution)/shard_map/ebrw,ewv->ebrv/dot_general | solution.py:83
  168.0 2.5 %convolution_convert_fusion.3 = bf16[4,6,8,512]{3,2,1,0:T(8,128)(2,1)S(1)} fusion(bf16[4,512,1022]{2,1,0:T(8,128)(2,1)} %reshape.39, f32[4,6,8,512]{3,2,1,0:T(8,128)S(1)} %convolution_subtract_fusion), kind=kOutput, calls=%fused_computation.55 | convolution fusion | flops 100859904 | bytes 2686976 | tf_op jit(solution)/shard_map/ebrv,ewv->ebrw/dot_general | solution.py:87
  170.5 2.3 %fusion.2 = f32[4,6,8,512]{3,2,1,0:T(8,128)S(1)} fusion(bf16[4,6,8,512]{3,2,1,0:T(8,128)(2,1)S(1)} %convolution_convert_fusion.3, bf16[4,1,512,512]{3,2,1,0:T(8,128)(2,1)} %copy.86), kind=kOutput, calls=%fused_computation.4 | convolution fusion | flops 100663296 | bytes 2686976 | tf_op jit(solution)/shard_map/ebrv,ewv->ebrw/dot_general | solution.py:95
  178.4 1.7 collective-permute-start.3
  180.1 5.4 %collective-permute-done.3 = bf16[4,6,8,512]{3,0,2,1:T(4,128)(2,1)S(1)} collective-permute-done((bf16[4,6,8,512]{3,0,2,1:T(4,128)(2,1)S(1)}, bf16[4,6,8,512]{3,0,2,1:T(4,128)(2,1)S(1)}, u32[]{:S(2)}, u32[]{:S(2)}) %collective-permute-start.3) | collective-permute-done | bytes 196640 | tf_op jit(solution)/shard_map/ppermute | solution.py:13
  186.3 22.3 %reduce-scatter.9.cloned.1.call-done = bf16[1,6,8,512]{3,2,1,0:T(8,128)(2,1)} async-done(((bf16[4,6,8,512]{3,2,1,0:T(8,128)(2,1)}), bf16[1,6,8,512]{3,2,1,0:T(8,128)(2,1)}) %reduce-scatter.9.cloned.1.call-update) | async-done | bytes 49168
  208.6 1.5 multiply_add_fusion
  (80 shorter events, 21.0 us)
Async XLA Ops:
  7.2 139.7 %reduce-scatter.7.cloned.1.call-start = ((), (), s32[]{:S(2)}) async-start(), calls=%async_computation.2 | async-start | bytes 245760
  18.4 81.3 %collective-permute-start = (bf16[4,6,8,512]{3,0,2,1:T(4,128)(2,1)S(1)}, bf16[4,6,8,512]{3,0,2,1:T(4,128)(2,1)S(1)}, u32[]{:S(2)}, u32[]{:S(2)}) collective-permute-start(bf16[4,6,8,512]{3,0,2,1:T(4,128)(2,1)S(1)} %copy.47), channel_id=1, source_target_pairs={{4,0},{8,4},{12,8},{16,12},{20,16},{24,20},{28,24},{0,28},{5,1},{9... | collective-permute-start | bytes 589832 | tf_op jit(solution)/shard_map/ppermute | solution.py:13
  59.5 2.0 copy-start.15
  59.5 2.0 copy-start.14
  59.5 2.1 copy-start.13
  101.9 1.6 copy-start
  102.4 1.9 copy-start.3
  104.0 1.7 copy-start.7
  104.7 1.4 copy-start.12
  109.4 3.2 %copy-start.4 = (bf16[4,1,512,512]{3,2,1,0:T(8,128)(2,1)S(1)}, bf16[4,1,512,512]{3,2,1,0:T(8,128)(2,1)}, u32[]{:S(2)}) copy-start(bf16[4,1,512,512]{3,2,1,0:T(8,128)(2,1)} %copy.84) | copy-start | bytes 6291460
  111.9 1.6 copy-start.8
  116.5 30.3 %copy-start.10 = (f32[1,6,8,512]{3,2,1,0:T(8,128)S(1)}, f32[1,6,8,512]{3,2,1,0:T(8,128)}, u32[]{:S(2)}) copy-start(f32[1,6,8,512]{3,2,1,0:T(8,128)} %param.8) | copy-start | bytes 294916
  117.4 6.9 %collective-permute-start.1 = (bf16[4,6,8,512]{3,0,2,1:T(4,128)(2,1)S(1)}, bf16[4,6,8,512]{3,0,2,1:T(4,128)(2,1)S(1)}, u32[]{:S(2)}, u32[]{:S(2)}) collective-permute-start(bf16[4,6,8,512]{3,0,2,1:T(4,128)(2,1)S(1)} %slice.164), channel_id=1, source_target_pairs={{28,0},{0,4},{4,8},{8,12},{12,16},{16,20},{20,24},{24,28},{29,1},{... | collective-permute-start | bytes 589832 | tf_op jit(solution)/shard_map/ppermute | solution.py:13
  125.2 83.4 %reduce-scatter.9.cloned.1.call-start = ((), (), s32[]{:S(2)}) async-start(), calls=%async_computation.3 | async-start | bytes 245760
  156.7 3.6 %collective-permute-start.2 = (bf16[4,6,8,512]{3,0,2,1:T(4,128)(2,1)S(1)}, bf16[4,6,8,512]{3,0,2,1:T(4,128)(2,1)S(1)}, u32[]{:S(2)}, u32[]{:S(2)}) collective-permute-start(bf16[4,6,8,512]{3,0,2,1:T(4,128)(2,1)S(1)} %copy.56), channel_id=1, source_target_pairs={{4,0},{8,4},{12,8},{16,12},{20,16},{24,20},{28,24},{0,28},{5,1},{9... | collective-permute-start | bytes 589832 | tf_op jit(solution)/shard_map/ppermute | solution.py:13
  162.2 1.6 copy-start.1
  162.6 1.9 copy-start.5
  168.0 4.8 %copy-start.9 = (f32[4,6,8,512]{3,2,1,0:T(8,128)}, f32[4,6,8,512]{3,2,1,0:T(8,128)S(1)}, u32[]{:S(2)}) copy-start(f32[4,6,8,512]{3,2,1,0:T(8,128)S(1)} %convolution_subtract_fusion) | copy-start | bytes 1179652
  168.0 4.8 %copy-start.6 = (bf16[4,1,512,512]{3,2,1,0:T(8,128)(2,1)S(1)}, bf16[4,1,512,512]{3,2,1,0:T(8,128)(2,1)}, u32[]{:S(2)}) copy-start(bf16[4,1,512,512]{3,2,1,0:T(8,128)(2,1)} %copy.84) | copy-start | bytes 6291460
  172.9 1.6 copy-start.2
  177.5 31.1 %copy-start.11 = (bf16[1,6,8,512]{3,2,1,0:T(8,128)(2,1)S(1)}, bf16[1,6,8,512]{3,2,1,0:T(8,128)(2,1)}, u32[]{:S(2)}) copy-start(bf16[1,6,8,512]{3,2,1,0:T(8,128)(2,1)} %reduce-scatter.7.cloned.1.call-done) | copy-start | bytes 147460
  178.4 7.1 %collective-permute-start.3 = (bf16[4,6,8,512]{3,0,2,1:T(4,128)(2,1)S(1)}, bf16[4,6,8,512]{3,0,2,1:T(4,128)(2,1)S(1)}, u32[]{:S(2)}, u32[]{:S(2)}) collective-permute-start(bf16[4,6,8,512]{3,0,2,1:T(4,128)(2,1)S(1)} %slice.163), channel_id=1, source_target_pairs={{28,0},{0,4},{4,8},{8,12},{12,16},{16,20},{20,24},{24,28},{29,1},{... | collective-permute-start | bytes 589832 | tf_op jit(solution)/shard_map/ppermute | solution.py:13
Sparse Core Ops, SparseCore 0:
  125.3 21.4 reduce-scatter.6
  186.5 22.0 reduce-scatter.8
where the time goes:
time: 218 us; the launch traced here: 217 us
  local copies, waits for them, and re-layouts  78.7 us (36%)
  waiting for transfers between devices  59.4 us (27%)
  matrix products  38.2 us (18%)
  blocking collectives  19.1 us (9%)
  between operations  14.5 us (7%)
  other arithmetic  3.8 us (2%)
  starting transfers between devices  3.34 us (2%)
    unnamed x4, waiting for transfers between devices  43.9 us
    unnamed x39, local copies, waits for them, and re-layouts  25.5 us
    slice x1, local copies, waits for them, and re-layouts, shards(): matrices[:, k]  24.7 us
    all_gather x2, blocking collectives, fetch_window(): own_group = lax.all_gather(sky_half, 'exp', axis=0, tiled=True)  19.1 us
    ppermute x4, waiting for transfers between devices, shifted(): return lax.ppermute(block, axis, route)  15.5 us
    dot_general x1, matrix products, shards(): jnp.einsum('ekn,nwv->ekwv', pick_res, resample_table, preferred_element_t...  10.1 us
    reshape x1, local copies, waits for them, and re-layouts, conv_matrices(): tiled[:, :width * (2 * width - 2)].reshape(count, width, 2 * width - 2)  9.37 us
    dot_general x8, matrix products, shards(): jnp.einsum('ebrv,ewv->ebrw', back, matrices[:, k], preferred_element_type...  9.1 us
  transfers between devices with their start and end apart: 6, of which 5 were waited for; matrix products, arithmetic and copies ran while one was open for 37% of the time, Pallas kernels for 0%

commit v1 on v0

--- a/solution.py
+++ b/solution.py
@@ -5,6 +5,28 @@
 
 ITERS = 2
 STEP = 0.05
+
+
+def laid_out(tiles, dim):
+    shape = list(tiles.shape[1:])
+    shape[dim] *= tiles.shape[0]
+    return jnp.moveaxis(tiles, 0, dim).reshape(shape)
+
+
+def collect(array, axis, dim):
+    count = lax.axis_size(axis)
+    pairs = [(i, (i + 1) % count) for i in range(count)]
+    back = [(b, a) for a, b in pairs]
+    lower, upper = ([], [])
+    for step in range(count - 1):
+        if step % 2 == 0:
+            lower.append(lax.ppermute(lower[-1] if lower else array, axis, pairs))
+        else:
+            upper.append(lax.ppermute(upper[-1] if upper else array, axis, back))
+    tiles = jnp.stack([*lower[::-1], array, *upper])
+    shift = lax.axis_index(axis) - len(lower)
+    tiles = tiles[(jnp.arange(count) - shift) % count]
+    return laid_out(tiles, dim)
 
 
 def shifted(block, axis, distance):
@@ -28,7 +50,7 @@
 
 
 def fetch_window(sky_half):
-    own_group = lax.all_gather(sky_half, "exp", axis=0, tiled=True)
+    own_group = collect(sky_half, "exp", 0)
     next_group = shifted(own_group, "grp", -1)
     return jnp.concatenate([own_group, next_group], axis=0)
 

time: 218 us -> 227 us (1.041)
  blocking collectives: 19.1 us -> 0 us
  waiting for transfers between devices: 59.4 us -> 69.7 us
  starting transfers between devices: 3.34 us -> 13.6 us
  local copies, waits for them, and re-layouts: 78.7 us -> 85.4 us
    all_gather x2 -> x0, blocking collectives: 19.1 us -> none  [fetch_window(): own_group = lax.all_gather(sky_half, 'exp', axis=0, tiled=True)]
    ppermute x0 -> x6, starting transfers between devices: none -> 8.83 us  [the longest x4 6.3 us: collect(): lower.append(lax.ppermute(lower[-1] if lower else array, axis, pairs))]
    ppermute x0 -> x6, waiting for transfers between devices: none -> 6.4 us  [the longest x4 6.39 us: collect(): lower.append(lax.ppermute(lower[-1] if lower else array, axis, pairs))]
    unnamed x39 -> x47, local copies, waits for them, and re-layouts: 25.5 us -> 29.6 us
    ppermute x4, waiting for transfers between devices: 15.5 us -> 18.7 us  [shifted(): return lax.ppermute(block, axis, route)]
  transfers between devices with their start and end apart: 6 -> 12, of which waited for: 5 -> 8; matrix products, arithmetic and copies ran while one was open for 37% -> 37% of each run, Pallas kernels for 0% -> 0%
where the time goes in v1:
time: 227 us; the launch traced here: 226 us
  local copies, waits for them, and re-layouts  85.4 us (38%)
  waiting for transfers between devices  69.7 us (31%)
  matrix products  38.3 us (17%)
  between operations  14.5 us (6%)
  starting transfers between devices  13.6 us (6%)
  other arithmetic  4.77 us (2%)
    unnamed x4, waiting for transfers between devices  44.6 us
    unnamed x47, local copies, waits for them, and re-layouts  29.6 us
    slice x1, local copies, waits for them, and re-layouts, shards(): matrices[:, k]  26.6 us
    ppermute x4, waiting for transfers between devices, shifted(): return lax.ppermute(block, axis, route)  18.7 us
    dot_general x1, matrix products, shards(): jnp.einsum('ekn,nwv->ekwv', pick_res, resample_table, preferred_element_t...  10.2 us
    reshape x1, local copies, waits for them, and re-layouts, conv_matrices(): tiled[:, :width * (2 * width - 2)].reshape(count, width, 2 * width - 2)  9.34 us
    dot_general x8, matrix products, shards(): jnp.einsum('ebrv,ewv->ebrw', back, matrices[:, k], preferred_element_type...  9.1 us
    ppermute x4, waiting for transfers between devices, collect(): lower.append(lax.ppermute(lower[-1] if lower else array, axis, pairs))  6.39 us
  transfers between devices with their start and end apart: 12, of which 8 were waited for; matrix products, arithmetic and copies ran while one was open for 37% of the time, Pallas kernels for 0%

profile of v1, /device:TPU:0, one launch (start us, length us, event | category | flops | bytes accessed | tf_op | source)
XLA Modules:
  0.0 226.2 jit_solution(9839091625931382023)
XLA Ops:
  8.1 2.9 %collective-permute-start = (bf16[1,6,8,512]{3,2,1,0:T(8,128)(2,1)S(1)}, bf16[1,6,8,512]{3,2,1,0:T(8,128)(2,1)S(1)}, u32[]{:S(2)}, u32[]{:S(2)}) collective-permute-start(bf16[1,6,8,512]{3,2,1,0:T(8,128)(2,1)S(1)} %convert_element_type.69), channel_id=1, source_target_pairs={{0,1},{1,2},{2,3},{3,0},{4,5},{5,6},{6,7},{7,4},{8,9},{9,10},{10,1... | collective-permute-start | bytes 147464 | tf_op jit(solution)/shard_map/ppermute | solution.py:23
  13.0 10.2 %convolution_convert_fusion = bf16[4,4,512,512]{3,1,2,0:T(4,128)(2,1)} fusion(bf16[8,512,512]{2,1,0:T(8,128)(2,1)} %param.13, s32[4,4]{1,0:T(4,128)} %param.11), kind=kOutput, calls=%fused_computation.2 | convolution fusion | flops 71303296 | bytes 12582976 | tf_op jit(solution)/shard_map/ekn,nwv->ekwv/dot_general | solution.py:90
  23.1 26.6 %fusion.109 = (bf16[4,1,512,512]{3,1,2,0:T(2,128)(2,1)}, bf16[4,1,512,512]{3,1,2,0:T(2,128)(2,1)}, bf16[4,1,512,512]{3,1,2,0:T(2,128)(2,1)}, bf16[4,1,512,512]{3,1,2,0:T(2,128)(2,1)}) fusion(bf16[4,4,512,512]{3,1,2,0:T(4,128)(2,1)} %convolution_convert_fusion), kind=kLoop, calls=%fused_computation.129 | loop fusion | bytes 16777216 | tf_op jit(solution)/shard_map/slice | solution.py:103
  51.9 3.0 %copy.170 = bf16[4,1,512,512]{3,2,1,0:T(8,128)(2,1)S(1)} copy(bf16[4,1,512,512]{3,1,2,0:T(2,128)(2,1)} %get-tuple-element.14) | data formatting | bytes 4194304
  55.3 2.0 copy.168
  58.2 1.9 copy.172
  61.2 1.9 copy.174
  63.1 2.5 %broadcast_in_dim.5 = bf16[4,512,1023]{2,1,0:T(8,128)(2,1)} broadcast(bf16[4,1023]{1,0:T(4,128)(2,1)S(1)} %maximum_convert_fusion), dimensions={0,2} | broadcast | bytes 4198392 | tf_op jit(solution)/shard_map/broadcast_in_dim | solution.py:45
  65.6 8.6 %reshape.140 = bf16[2095104]{0:T(1024)(128)(2,1)} reshape(bf16[4,512,1023]{2,1,0:T(8,128)(2,1)} %broadcast_in_dim.5) | data formatting | bytes 8380416
  74.1 5.7 %reshape.94 = bf16[4,523776]{1,0:T(4,128)(2,1)} reshape(bf16[2095104]{0:T(1024)(128)(2,1)} %reshape.140) | data formatting | bytes 8380416 | tf_op jit(solution)/shard_map/reshape | solution.py:45
  79.8 5.4 %slice.129 = bf16[4,523264]{1,0:T(4,128)(2,1)} slice(bf16[4,523776]{1,0:T(4,128)(2,1)} %reshape.94), slice={[0:4], [0:523264]} | slice | bytes 8372224 | tf_op jit(solution)/shard_map/slice | solution.py:48
  85.2 5.7 %reshape.142 = bf16[2093056]{0:T(1024)(128)(2,1)} reshape(bf16[4,523264]{1,0:T(4,128)(2,1)} %slice.129) | data formatting | bytes 8372224
  90.9 9.3 %reshape.95 = bf16[4,512,1022]{2,1,0:T(8,128)(2,1)} reshape(bf16[2093056]{0:T(1024)(128)(2,1)} %reshape.142) | data formatting | bytes 8372224 | tf_op jit(solution)/shard_map/reshape | solution.py:48
  101.0 2.5 %collective-permute-start.3 = (bf16[4,6,8,512]{3,0,2,1:T(4,128)(2,1)S(1)}, bf16[4,6,8,512]{3,0,2,1:T(4,128)(2,1)S(1)}, u32[]{:S(2)}, u32[]{:S(2)}) collective-permute-start(bf16[4,6,8,512]{3,0,2,1:T(4,128)(2,1)S(1)} %copy.131), channel_id=1, source_target_pairs={{4,0},{8,4},{12,8},{16,12},{20,16},{24,20},{28,24},{0,28},{5,1},{9... | collective-permute-start | bytes 589832 | tf_op jit(solution)/shard_map/ppermute | solution.py:35
  103.6 3.1 %collective-permute-done.3 = bf16[4,6,8,512]{3,0,2,1:T(4,128)(2,1)S(1)} collective-permute-done((bf16[4,6,8,512]{3,0,2,1:T(4,128)(2,1)S(1)}, bf16[4,6,8,512]{3,0,2,1:T(4,128)(2,1)S(1)}, u32[]{:S(2)}, u32[]{:S(2)}) %collective-permute-start.3) | collective-permute-done | bytes 196640 | tf_op jit(solution)/shard_map/ppermute | solution.py:35
  107.1 1.7 fusion.111
  113.0 3.4 %convolution_convert_fusion.4 = bf16[4,6,8,512]{3,2,1,0:T(8,128)(2,1)S(1)} fusion(bf16[4,6,8,512]{3,2,1,0:T(8,128)(2,1)S(1)} %fusion.56, bf16[4,512,1022]{2,1,0:T(8,128)(2,1)} %reshape.95, bf16[4,6,8,512]{3,2,1,0:T(8,128)(2,1)S(1)} %copy-done.15), kind=kOutput, calls=%fused_computation.58 | convolution fusion | flops 201719808 | bytes 4775936 | tf_op jit(solution)/shard_map/ebrv,ewv->ebrw/dot_general | solution.py:109
  116.4 2.5 %fusion.30 = f32[4,6,8,512]{3,2,1,0:T(8,128)S(1)} fusion(bf16[4,6,8,512]{3,2,1,0:T(8,128)(2,1)S(1)} %convolution_convert_fusion.4, bf16[4,1,512,512]{3,2,1,0:T(8,128)(2,1)} %copy.168), kind=kOutput, calls=%fused_computation.34 | convolution fusion | flops 100663296 | bytes 2686976 | tf_op jit(solution)/shard_map/ebrv,ewv->ebrw/dot_general | solution.py:117
  124.5 7.1 %collective-permute-done.4 = bf16[4,6,8,512]{3,0,2,1:T(4,128)(2,1)S(1)} collective-permute-done((bf16[4,6,8,512]{3,0,2,1:T(4,128)(2,1)S(1)}, bf16[4,6,8,512]{3,0,2,1:T(4,128)(2,1)S(1)}, u32[]{:S(2)}, u32[]{:S(2)}) %collective-permute-start.4) | collective-permute-done | bytes 196640 | tf_op jit(solution)/shard_map/ppermute | solution.py:35
  132.4 22.3 %reduce-scatter.7.cloned.1.call-done = bf16[1,6,8,512]{3,2,1,0:T(8,128)(2,1)} async-done(((bf16[4,6,8,512]{3,2,1,0:T(8,128)(2,1)}), bf16[1,6,8,512]{3,2,1,0:T(8,128)(2,1)}) %reduce-scatter.7.cloned.1.call-update) | async-done | bytes 49168
  155.5 1.5 collective-permute-start.5
  157.0 1.5 collective-permute-start.7
  158.5 2.1 collective-permute-done.5
  161.2 4.3 %collective-permute-done.6 = bf16[1,6,8,512]{3,2,1,0:T(8,128)(2,1)S(1)} collective-permute-done((bf16[1,6,8,512]{3,2,1,0:T(8,128)(2,1)S(1)}, bf16[1,6,8,512]{3,2,1,0:T(8,128)(2,1)S(1)}, u32[]{:S(2)}, u32[]{:S(2)}) %collective-permute-start.6) | collective-permute-done | bytes 49184 | tf_op jit(solution)/shard_map/ppermute | solution.py:23
  166.6 3.2 %collective-permute-done.8 = bf16[4,6,8,512]{3,0,2,1:T(4,128)(2,1)S(1)} collective-permute-done((bf16[4,6,8,512]{3,0,2,1:T(4,128)(2,1)S(1)}, bf16[4,6,8,512]{3,0,2,1:T(4,128)(2,1)S(1)}, u32[]{:S(2)}, u32[]{:S(2)}) %collective-permute-start.8) | collective-permute-done | bytes 196640 | tf_op jit(solution)/shard_map/ppermute | solution.py:35
  174.2 3.0 %convolution_subtract_fusion = f32[4,6,8,512]{3,2,1,0:T(8,128)S(1)} fusion(f32[4,6,8,512]{3,2,1,0:T(8,128)S(1)} %fusion.43, bf16[4,1,512,512]{3,2,1,0:T(8,128)(2,1)} %copy.174, bf16[4,512,1022]{2,1,0:T(8,128)(2,1)} %reshape.95, bf16[4,6,8,512]{3,2,1,0:T(8,128)(2,1)} %param.9, bf16[4,1,6,8,512]{4,1,3,2,0:T(2,128)(2,1)S(1)} %get-tuple-element.16), kind=kOutput, calls=%fused_computation.52 | convolution fusion | flops 201719808 | bytes 5373952 | tf_op jit(solution)/shard_map/ebrw,ewv->ebrv/dot_general | solution.py:105
  177.3 2.5 %convolution_convert_fusion.3 = bf16[4,6,8,512]{3,2,1,0:T(8,128)(2,1)S(1)} fusion(bf16[4,512,1022]{2,1,0:T(8,128)(2,1)} %reshape.95, f32[4,6,8,512]{3,2,1,0:T(8,128)S(1)} %convolution_subtract_fusion), kind=kOutput, calls=%fused_computation.57 | convolution fusion | flops 100859904 | bytes 2686976 | tf_op jit(solution)/shard_map/ebrv,ewv->ebrw/dot_general | solution.py:109
  179.8 2.3 %fusion.2 = f32[4,6,8,512]{3,2,1,0:T(8,128)S(1)} fusion(bf16[4,6,8,512]{3,2,1,0:T(8,128)(2,1)S(1)} %convolution_convert_fusion.3, bf16[4,1,512,512]{3,2,1,0:T(8,128)(2,1)} %copy.174), kind=kOutput, calls=%fused_computation.6 | convolution fusion | flops 100663296 | bytes 2686976 | tf_op jit(solution)/shard_map/ebrv,ewv->ebrw/dot_general | solution.py:117
  187.6 1.8 collective-permute-start.9
  189.4 5.3 %collective-permute-done.9 = bf16[4,6,8,512]{3,0,2,1:T(4,128)(2,1)S(1)} collective-permute-done((bf16[4,6,8,512]{3,0,2,1:T(4,128)(2,1)S(1)}, bf16[4,6,8,512]{3,0,2,1:T(4,128)(2,1)S(1)}, u32[]{:S(2)}, u32[]{:S(2)}) %collective-permute-start.9) | collective-permute-done | bytes 196640 | tf_op jit(solution)/shard_map/ppermute | solution.py:35
  195.6 22.3 %reduce-scatter.9.cloned.1.call-done = bf16[1,6,8,512]{3,2,1,0:T(8,128)(2,1)} async-done(((bf16[4,6,8,512]{3,2,1,0:T(8,128)(2,1)}), bf16[1,6,8,512]{3,2,1,0:T(8,128)(2,1)}) %reduce-scatter.9.cloned.1.call-update) | async-done | bytes 49168
  217.9 1.5 multiply_add_fusion
  (105 shorter events, 32.3 us)
Async XLA Ops:
  7.2 147.5 %reduce-scatter.7.cloned.1.call-start = ((), (), s32[]{:S(2)}) async-start(), calls=%async_computation.2 | async-start | bytes 245760
  8.1 42.4 %collective-permute-start = (bf16[1,6,8,512]{3,2,1,0:T(8,128)(2,1)S(1)}, bf16[1,6,8,512]{3,2,1,0:T(8,128)(2,1)S(1)}, u32[]{:S(2)}, u32[]{:S(2)}) collective-permute-start(bf16[1,6,8,512]{3,2,1,0:T(8,128)(2,1)S(1)} %convert_element_type.69), channel_id=1, source_target_pairs={{0,1},{1,2},{2,3},{3,0},{4,5},{5,6},{6,7},{7,4},{8,9},{9,10},{10,1... | collective-permute-start | bytes 147464 | tf_op jit(solution)/shard_map/ppermute | solution.py:23
  11.1 89.2 %collective-permute-start.2 = (bf16[1,6,8,512]{3,2,1,0:T(8,128)(2,1)S(1)}, bf16[1,6,8,512]{3,2,1,0:T(8,128)(2,1)S(1)}, u32[]{:S(2)}, u32[]{:S(2)}) collective-permute-start(bf16[1,6,8,512]{3,2,1,0:T(8,128)(2,1)S(1)} %convert_element_type.69), channel_id=1, source_target_pairs={{1,0},{2,1},{3,2},{0,3},{5,4},{6,5},{7,6},{4,7},{9,8},{10,9},{11,1... | collective-permute-start | bytes 147464 | tf_op jit(solution)/shard_map/ppermute | solution.py:25
  23.1 26.7 %copy-start.19 = (s32[4]{0:T(128)S(1)}, s32[4]{0:T(128)}, u32[]{:S(2)}) copy-start(s32[4]{0:T(128)} %param.12) | copy-start | bytes 52
  23.1 26.7 %copy-start.17 = (f32[16,8]{0,1:T(8,128)S(1)}, f32[16,8]{0,1:T(8,128)}, u32[]{:S(2)}) copy-start(f32[16,8]{0,1:T(8,128)} %param.14) | copy-start | bytes 1540
  23.1 26.8 %copy-start.16 = (f32[8,41]{1,0:T(8,128)S(1)}, f32[8,41]{1,0:T(8,128)}, u32[]{:S(2)}) copy-start(f32[8,41]{1,0:T(8,128)} %param.15) | copy-start | bytes 3940
  23.1 28.6 %copy-start.18 = (s32[4,4]{1,0:T(4,128)S(1)}, s32[4,4]{1,0:T(4,128)}, u32[]{:S(2)}) copy-start(s32[4,4]{1,0:T(4,128)} %param.10) | copy-start | bytes 196
  50.5 49.8 %collective-permute-start.1 = (bf16[1,6,8,512]{3,2,1,0:T(8,128)(2,1)S(1)}, bf16[1,6,8,512]{3,2,1,0:T(8,128)(2,1)S(1)}, u32[]{:S(2)}, u32[]{:S(2)}) collective-permute-start(bf16[1,6,8,512]{3,2,1,0:T(8,128)(2,1)S(1)} %collective-permute-done), channel_id=1, source_target_pairs={{0,1},{1,2},{2,3},{3,0},{4,5},{5,6},{6,7},{7,4},{8,9},{9,10},{10,1... | collective-permute-start | bytes 147464 | tf_op jit(solution)/shard_map/ppermute | solution.py:23
  51.8 3.4 %copy-start.11 = (bf16[4,1,512,512]{3,1,2,0:T(2,128)(2,1)S(1)}, bf16[4,1,512,512]{3,1,2,0:T(2,128)(2,1)}, u32[]{:S(2)}) copy-start(bf16[4,1,512,512]{3,1,2,0:T(2,128)(2,1)} %get-tuple-element.15) | copy-start | bytes 6291460
  55.3 2.9 %copy-start.10 = (bf16[4,1,512,512]{3,1,2,0:T(2,128)(2,1)S(1)}, bf16[4,1,512,512]{3,1,2,0:T(2,128)(2,1)}, u32[]{:S(2)}) copy-start(bf16[4,1,512,512]{3,1,2,0:T(2,128)(2,1)} %get-tuple-element.13) | copy-start | bytes 6291460
  58.2 2.9 %copy-start.9 = (bf16[4,1,512,512]{3,1,2,0:T(2,128)(2,1)S(1)}, bf16[4,1,512,512]{3,1,2,0:T(2,128)(2,1)}, u32[]{:S(2)}) copy-start(bf16[4,1,512,512]{3,1,2,0:T(2,128)(2,1)} %get-tuple-element.12) | copy-start | bytes 6291460
  101.0 5.7 %collective-permute-start.3 = (bf16[4,6,8,512]{3,0,2,1:T(4,128)(2,1)S(1)}, bf16[4,6,8,512]{3,0,2,1:T(4,128)(2,1)S(1)}, u32[]{:S(2)}, u32[]{:S(2)}) collective-permute-start(bf16[4,6,8,512]{3,0,2,1:T(4,128)(2,1)S(1)} %copy.131), channel_id=1, source_target_pairs={{4,0},{8,4},{12,8},{16,12},{20,16},{24,20},{28,24},{0,28},{5,1},{9... | collective-permute-start | bytes 589832 | tf_op jit(solution)/shard_map/ppermute | solution.py:35
  108.9 1.6 copy-start
  109.3 1.9 copy-start.3
  110.9 1.7 copy-start.7
  111.7 1.4 copy-start.15
  116.4 3.2 %copy-start.4 = (bf16[4,1,512,512]{3,2,1,0:T(8,128)(2,1)S(1)}, bf16[4,1,512,512]{3,2,1,0:T(8,128)(2,1)}, u32[]{:S(2)}) copy-start(bf16[4,1,512,512]{3,2,1,0:T(8,128)(2,1)} %copy.172) | copy-start | bytes 6291460
  118.9 1.6 copy-start.8
  123.5 31.2 %copy-start.12 = (f32[1,6,8,512]{3,2,1,0:T(8,128)S(1)}, f32[1,6,8,512]{3,2,1,0:T(8,128)}, u32[]{:S(2)}) copy-start(f32[1,6,8,512]{3,2,1,0:T(8,128)} %param.8) | copy-start | bytes 294916
  124.4 7.1 %collective-permute-start.4 = (bf16[4,6,8,512]{3,0,2,1:T(4,128)(2,1)S(1)}, bf16[4,6,8,512]{3,0,2,1:T(4,128)(2,1)S(1)}, u32[]{:S(2)}, u32[]{:S(2)}) collective-permute-start(bf16[4,6,8,512]{3,0,2,1:T(4,128)(2,1)S(1)} %slice.168), channel_id=1, source_target_pairs={{28,0},{0,4},{4,8},{8,12},{12,16},{16,20},{20,24},{24,28},{29,1},{... | collective-permute-start | bytes 589832 | tf_op jit(solution)/shard_map/ppermute | solution.py:35
  132.4 85.5 %reduce-scatter.9.cloned.1.call-start = ((), (), s32[]{:S(2)}) async-start(), calls=%async_computation.3 | async-start | bytes 245760
  155.5 5.0 %collective-permute-start.5 = (bf16[1,6,8,512]{3,2,1,0:T(8,128)(2,1)S(1)}, bf16[1,6,8,512]{3,2,1,0:T(8,128)(2,1)S(1)}, u32[]{:S(2)}, u32[]{:S(2)}) collective-permute-start(bf16[1,6,8,512]{3,2,1,0:T(8,128)(2,1)S(1)} %fusion.97), channel_id=1, source_target_pairs={{0,1},{1,2},{2,3},{3,0},{4,5},{5,6},{6,7},{7,4},{8,9},{9,10},{10,1... | collective-permute-start | bytes 147464 | tf_op jit(solution)/shard_map/ppermute | solution.py:23
  157.0 4.2 %collective-permute-start.7 = (bf16[1,6,8,512]{3,2,1,0:T(8,128)(2,1)S(1)}, bf16[1,6,8,512]{3,2,1,0:T(8,128)(2,1)S(1)}, u32[]{:S(2)}, u32[]{:S(2)}) collective-permute-start(bf16[1,6,8,512]{3,2,1,0:T(8,128)(2,1)S(1)} %fusion.97), channel_id=1, source_target_pairs={{1,0},{2,1},{3,2},{0,3},{5,4},{6,5},{7,6},{4,7},{9,8},{10,9},{11,1... | collective-permute-start | bytes 147464 | tf_op jit(solution)/shard_map/ppermute | solution.py:25
  160.6 5.0 %collective-permute-start.6 = (bf16[1,6,8,512]{3,2,1,0:T(8,128)(2,1)S(1)}, bf16[1,6,8,512]{3,2,1,0:T(8,128)(2,1)S(1)}, u32[]{:S(2)}, u32[]{:S(2)}) collective-permute-start(bf16[1,6,8,512]{3,2,1,0:T(8,128)(2,1)S(1)} %collective-permute-done.5), channel_id=1, source_target_pairs={{0,1},{1,2},{2,3},{3,0},{4,5},{5,6},{6,7},{7,4},{8,9},{9,10},{10,1... | collective-permute-start | bytes 147464 | tf_op jit(solution)/shard_map/ppermute | solution.py:23
  166.3 3.5 %collective-permute-start.8 = (bf16[4,6,8,512]{3,0,2,1:T(4,128)(2,1)S(1)}, bf16[4,6,8,512]{3,0,2,1:T(4,128)(2,1)S(1)}, u32[]{:S(2)}, u32[]{:S(2)}) collective-permute-start(bf16[4,6,8,512]{3,0,2,1:T(4,128)(2,1)S(1)} %copy.144), channel_id=1, source_target_pairs={{4,0},{8,4},{12,8},{16,12},{20,16},{24,20},{28,24},{0,28},{5,1},{9... | collective-permute-start | bytes 589832 | tf_op jit(solution)/shard_map/ppermute | solution.py:35
  171.4 1.6 copy-start.1
  171.9 1.9 copy-start.5
  177.2 4.8 %copy-start.13 = (f32[4,6,8,512]{3,2,1,0:T(8,128)}, f32[4,6,8,512]{3,2,1,0:T(8,128)S(1)}, u32[]{:S(2)}) copy-start(f32[4,6,8,512]{3,2,1,0:T(8,128)S(1)} %convolution_subtract_fusion) | copy-start | bytes 1179652
  177.2 4.8 %copy-start.6 = (bf16[4,1,512,512]{3,2,1,0:T(8,128)(2,1)S(1)}, bf16[4,1,512,512]{3,2,1,0:T(8,128)(2,1)}, u32[]{:S(2)}) copy-start(bf16[4,1,512,512]{3,2,1,0:T(8,128)(2,1)} %copy.172) | copy-start | bytes 6291460
  182.1 1.6 copy-start.2
  186.7 31.2 %copy-start.14 = (bf16[1,6,8,512]{3,2,1,0:T(8,128)(2,1)S(1)}, bf16[1,6,8,512]{3,2,1,0:T(8,128)(2,1)}, u32[]{:S(2)}) copy-start(bf16[1,6,8,512]{3,2,1,0:T(8,128)(2,1)} %reduce-scatter.7.cloned.1.call-done) | copy-start | bytes 147460
  187.6 7.1 %collective-permute-start.9 = (bf16[4,6,8,512]{3,0,2,1:T(4,128)(2,1)S(1)}, bf16[4,6,8,512]{3,0,2,1:T(4,128)(2,1)S(1)}, u32[]{:S(2)}, u32[]{:S(2)}) collective-permute-start(bf16[4,6,8,512]{3,0,2,1:T(4,128)(2,1)S(1)} %slice.167), channel_id=1, source_target_pairs={{28,0},{0,4},{4,8},{8,12},{12,16},{16,20},{20,24},{24,28},{29,1},{... | collective-permute-start | bytes 589832 | tf_op jit(solution)/shard_map/ppermute | solution.py:35
Sparse Core Ops, SparseCore 0:
  132.5 22.1 reduce-scatter.6
  195.7 22.1 reduce-scatter.8
